TPU v7x, 512 devices: a whole 4x4x16 slice. The times are simulated.
512 devices in a mesh: pair: 64 (over z_lo, x, core), aux: 8 (over y, z_hi).
Axes of the slice: x: 4, y: 4, z: 16 (z_hi: 2, z_lo: 8; z = z_hi * 8 + z_lo), core: 2. Of those that a mesh axis runs over, the one named last changes fastest.
Arguments:
- doubles: bfloat16 [128, 512, 512], P('pair', 'aux'), may hold values from -1.796875 to 1.796875
- singles: bfloat16 [256, 512], replicated, may hold values from -0.8984375 to 0.8984375
- vir_slabs: bfloat16 [4096, 8, 512], P(('aux', 'pair')), may hold values from -0.059814453 to 0.059814453
- occ_slabs: bfloat16 [4096, 256, 512], P(('aux', 'pair')), may hold values from -0.029907227 to 0.029907227
- occ_energy: float32 [256], replicated, may hold values from -2 to -0.5
- vir_energy: float32 [8], replicated, may hold values from 0.1 to 1.5
- pair_list: int32 [128, 2], P('pair'), may hold values from 0 to 255
Outputs:
- new_doubles: float32 [128, 8, 8], P('pair', 'aux')
All inputs are finite; a program needn't handle non-finite values.
Results may differ from a plain program's by a relative error of at most 0.0005.
Values may be sent and summed in bfloat16 or wider, within the bound.
No kernel may reach another device: no remote copies, remote signals or barrier semaphores. Data moves between devices by JAX's collectives and lax.ppermute only.
A program may use at most 64 MiB of HBM per device.

v0:
```python
import math
import jax
import jax.numpy as jnp
from jax import lax
from jax.sharding import PartitionSpec as P

NWIN = 8


def ladder_block(running, slab_block, tau_amps):
    half_done = jnp.einsum(
        "qac,pcd->pqad", slab_block, tau_amps, preferred_element_type=jnp.float32
    ).astype(jnp.bfloat16)
    return running + jnp.einsum(
        "pqad,qbd->pab", half_done, slab_block, preferred_element_type=jnp.float32
    )


def ladder_rows(running, slab_piece, tau_amps):
    row_count = slab_piece.shape[0]
    block_size = math.gcd(row_count, 64)
    blocks = slab_piece.reshape(
        row_count // block_size, block_size, slab_piece.shape[1], slab_piece.shape[2]
    )

    def one_block(carried, slab_block):
        return (ladder_block(carried, slab_block, tau_amps), None)

    return lax.scan(one_block, running, blocks)[0]


def body(doubles, singles, vir_slabs, occ_slabs, occ_energy, vir_energy, pair_list):
    full_doubles = lax.all_gather(doubles, "aux", axis=1, tiled=True)
    first_occ = pair_list[:, 0]
    second_occ = pair_list[:, 1]
    occ_ids = lax.broadcasted_iota(jnp.int32, (pair_list.shape[0], singles.shape[0]), 1)
    match_first = first_occ[:, None] == occ_ids
    match_second = second_occ[:, None] == occ_ids
    row_first = jnp.dot(
        match_first.astype(jnp.bfloat16), singles, preferred_element_type=jnp.float32
    )
    row_second = jnp.dot(
        match_second.astype(jnp.bfloat16), singles, preferred_element_type=jnp.float32
    )
    tau_amps = (
        full_doubles.astype(jnp.float32) + row_first[:, :, None] * row_second[:, None, :]
    ).astype(jnp.bfloat16)
    dressing_cols = singles[:, :NWIN]
    dressed = (
        vir_slabs.astype(jnp.float32)
        - jnp.einsum("ka,qkc->qac", dressing_cols, occ_slabs, preferred_element_type=jnp.float32)
    ).astype(jnp.bfloat16)
    local_pairs = tau_amps.shape[0]
    empty = jnp.zeros((local_pairs, NWIN, NWIN), jnp.float32)
    gathered = lax.all_gather(dressed, "pair", axis=0, tiled=True)
    partial_value = ladder_rows(empty, gathered, tau_amps)
    share = lax.psum_scatter(partial_value, "aux", scatter_dimension=1, tiled=True)
    share_rows = NWIN // lax.axis_size("aux")
    row_start = lax.axis_index("aux") * share_rows
    own_doubles = lax.dynamic_slice_in_dim(full_doubles[:, :NWIN, :NWIN], row_start, share_rows, 1)
    own_vir = lax.dynamic_slice_in_dim(vir_energy, row_start, share_rows, 0)
    energy_first = jnp.sum(jnp.where(match_first, occ_energy[None, :], 0.0), axis=1)
    energy_second = jnp.sum(jnp.where(match_second, occ_energy[None, :], 0.0), axis=1)
    pair_energy = energy_first + energy_second
    denominator = pair_energy[:, None, None] - own_vir[None, :, None] - vir_energy[None, None, :]
    return own_doubles.astype(jnp.float32) + share / denominator


def solution(mesh):
    placed = (
        P("pair", "aux", None),
        P(),
        P(("aux", "pair"), None, None),
        P(("aux", "pair"), None, None),
        P(),
        P(),
        P("pair", None),
    )
    return jax.shard_map(
        body, mesh=mesh, in_specs=placed, out_specs=P("pair", "aux", None), check_vma=False
    )
```

profile of v0, /device:TPU:32, one launch (start us, length us, event | category | flops | bytes accessed | tf_op | source)
XLA Modules:
  0.0 289.2 jit_solution(11236321871546542226)
XLA Ops:
  6.5 0.0 copy-start
  6.5 0.0 copy-start.1
  6.5 0.0 copy-start.4
  6.5 0.0 copy-start.2
  6.5 0.0 copy-start.3
  6.5 0.0 all-gather.3.cloned.1.call-start
  6.6 1.8 copy.21
  8.4 0.0 all-gather.3.cloned.1.call-update
  8.4 0.0 all-gather.5.cloned.1.call-start
  8.5 0.0 copy-done
  8.5 1.9 fusion.13
  10.4 0.0 all-gather.5.cloned.1.call-update
  10.5 0.0 copy-done.4
  10.5 0.6 dynamic_slice.11
  11.1 1.3 dynamic-slice
  12.4 0.0 copy-done.2
  12.4 0.2 slice_reduce_fusion.1
  12.6 0.0 copy-done.3
  12.6 0.2 select_reduce_fusion
  12.8 0.6 add_subtract_fusion
  13.5 0.0 copy-done.1
  13.5 0.2 fusion.16
  13.7 0.3 fusion.17
  13.9 84.6 %all-gather.3.cloned.1.call-done = bf16[2,512,512]{2,0,1:T(2,128)(2,1)} async-done(((bf16[2,64,512]{2,0,1:T(2,128)(2,1)}), bf16[2,512,512]{2,0,1:T(2,128)(2,1)}) %all-gather.3.cloned.1.call-update) | async-done | bytes 1048592 | tf_op jit(solution)/shard_map/all_gather | solution.py:33
  98.6 2.3 add_convert_fusion
  100.9 0.2 copy.24
  101.1 0.7 slice.16
  101.7 119.4 %all-gather.5.cloned.1.call-done = bf16[512,8,512]{2,1,0:T(8,128)(2,1)} async-done(((bf16[8,8,512]{2,1,0:T(8,128)(2,1)}), bf16[512,8,512]{2,1,0:T(8,128)(2,1)}) %all-gather.5.cloned.1.call-update) | async-done | bytes 4194320 | tf_op jit(solution)/shard_map/all_gather | solution.py:55
  221.1 17.7 %while.11 = (s32[]{:T(128)}, f32[2,8,8]{2,1,0:T(8,128)S(1)}, bf16[8,64,8,512]{3,2,1,0:T(8,128)(2,1)}, bf16[2,512,512]{2,1,0:T(8,128)(2,1)S(1)}, s32[]{:T(128)}, /*index=5*/s32[]{:T(128)}) while((s32[]{:T(128)}, f32[2,8,8]{2,1,0:T(8,128)S(1)}, bf16[8,64,8,512]{3,2,1,0:T(8,128)(2,1)}, bf16[2,512,512]{2,1,0:T(8,128)(2,1)S(1)}, ...), condition=%wide.region_1.2_spmd.clone, body=%wide.region_0.1_spmd.clone.sunk | while | flops 545784064 | bytes 2099279 | solution.py:29
  221.1 2.2 fusion.31
  223.3 2.2 fusion.31
  225.5 2.2 fusion.31
  227.7 2.2 fusion.31
  230.0 2.2 fusion.31
  232.2 2.2 fusion.31
  234.4 2.2 fusion.31
  236.6 2.2 fusion.31
  238.8 42.2 %all-reduce = f32[2,8,8]{2,0,1:T(2,128)S(1)} all-reduce(f32[2,8,8]{2,0,1:T(2,128)S(1)} %copy.25), channel_id=2, replica_groups=mesh['pair'=64,'aux'=8] {'aux'}, use_global_device_ids=true, to_apply=%region_2.3.clone | all-reduce | flops 128 | bytes 1024
  281.1 1.3 fusion.20
  (2 shorter events, 0.0 us)
Async XLA Ops:
  6.5 2.0 copy-start
  6.5 6.9 %copy-start.1 = (bf16[256,512]{1,0:T(8,128)(2,1)S(1)}, bf16[256,512]{1,0:T(8,128)(2,1)}, u32[]{:S(2)}) copy-start(bf16[256,512]{1,0:T(8,128)(2,1)} %param.10) | copy-start | bytes 786436
  6.5 3.9 %copy-start.4 = (f32[8]{0:T(128)S(1)}, f32[8]{0:T(128)}, u32[]{:S(2)}) copy-start(f32[8]{0:T(128)} %param.14) | copy-start | bytes 100
  6.5 5.9 %copy-start.2 = (s32[2,2]{1,0:T(2,128)S(1)}, s32[2,2]{1,0:T(2,128)}, u32[]{:S(2)}) copy-start(s32[2,2]{1,0:T(2,128)} %param.15) | copy-start | bytes 52
  6.5 6.1 %copy-start.3 = (f32[256]{0:T(256)S(1)}, f32[256]{0:T(256)}, u32[]{:S(2)}) copy-start(f32[256]{0:T(256)} %param.13) | copy-start | bytes 3076
  6.5 92.0 %all-gather.3.cloned.1.call-start = ((), (), s32[]{:S(2)}) async-start(), calls=%async_computation | async-start | bytes 1179648 | tf_op jit(solution)/shard_map/all_gather | solution.py:33
  8.4 212.7 %all-gather.5.cloned.1.call-start = ((), (), s32[]{:S(2)}) async-start(), calls=%async_computation.1 | async-start | bytes 4259840 | tf_op jit(solution)/shard_map/all_gather | solution.py:55
Sparse Core Ops, SparseCore 0:
  10.6 87.9 all-gather.2
  100.7 120.3 all-gather.4
where the time goes:
time: 290 us; the launch traced here: 289 us
  waiting for transfers between devices  204 us (70%)
  blocking collectives  42.2 us (15%)
  matrix products  19.9 us (7%)
  between operations  13.5 us (5%)
  local copies, waits for them, and re-layouts  4.82 us (2%)
  other arithmetic  4.42 us (2%)
    all_gather x1, waiting for transfers between devices, body(): gathered = lax.all_gather(dressed, 'pair', axis=0, tiled=True)  119 us
    all_gather x1, waiting for transfers between devices, body(): full_doubles = lax.all_gather(doubles, 'aux', axis=1, tiled=True)  84.6 us
    unnamed x1, blocking collectives  42.2 us
    dot_general x8, matrix products, ladder_block(): jnp.einsum('pqad,qbd->pab', half_done, slab_block, preferred_element_type...  17.5 us
  transfers between devices with their start and end apart: 2, of which 2 were waited for; matrix products, arithmetic and copies ran while one was open for 3% of the time, Pallas kernels for 0%

commit v1 on v0

--- a/solution.py
+++ b/solution.py
@@ -30,7 +30,9 @@
 
 
 def body(doubles, singles, vir_slabs, occ_slabs, occ_energy, vir_energy, pair_list):
-    full_doubles = lax.all_gather(doubles, "aux", axis=1, tiled=True)
+    full_doubles = jnp.concatenate(
+        lax.all_to_all(jnp.stack([doubles] * lax.axis_size("aux")), "aux", 0, 0), axis=1
+    )
     first_occ = pair_list[:, 0]
     second_occ = pair_list[:, 1]
     occ_ids = lax.broadcasted_iota(jnp.int32, (pair_list.shape[0], singles.shape[0]), 1)

time: 290 us -> 243 us (0.84)
  the two profiles are of different devices: /device:TPU:32 before, /device:TPU:36 now
where the time goes in v1:
time: 243 us
  waiting for transfers between devices  142 us (58%)
  blocking collectives  43 us (18%)
  matrix products  19.8 us (8%)
  starting transfers between devices  16.8 us (7%)
  between operations  13.5 us (6%)
  local copies, waits for them, and re-layouts  4.83 us (2%)
    all_gather x1, waiting for transfers between devices, body(): gathered = lax.all_gather(dressed, 'pair', axis=0, tiled=True)  87.2 us
    all_to_all x1, waiting for transfers between devices, body(): lax.all_to_all(jnp.stack([doubles] * lax.axis_size('aux')), 'aux', 0, 0)  54.8 us
    unnamed x1, blocking collectives  43 us
    dot_general x8, matrix products, ladder_block(): jnp.einsum('pqad,qbd->pab', half_done, slab_block, preferred_element_type...  17.5 us
    all_to_all x1, starting transfers between devices, body(): lax.all_to_all(jnp.stack([doubles] * lax.axis_size('aux')), 'aux', 0, 0)  16.8 us
  transfers between devices with their start and end apart: 2, of which 2 were waited for; matrix products, arithmetic and copies ran while one was open for 2% of the time, Pallas kernels for 0%

profile of v1, /device:TPU:36, one launch (start us, length us, event | category | flops | bytes accessed | tf_op | source)
XLA Modules:
  0.0 242.6 jit_solution(7728252992855049520)
XLA Ops:
  6.5 0.0 copy-start
  6.5 0.0 copy-start.1
  6.5 0.0 all-gather.2.cloned.1.call-start
  6.5 1.6 copy-done
  8.1 1.9 fusion.13
  10.0 0.0 copy-start.5
  10.0 0.0 copy-start.3
  10.0 0.0 copy-start.4
  10.1 0.0 copy-start.2
  10.1 0.0 all-gather.2.cloned.1.call-update
  10.1 0.0 copy-done.1
  10.1 1.1 stack.2
  11.2 16.8 %all-to-all-start = ((bf16[8,2,64,512]{3,2,1,0:T(8,128)(2,1)}), bf16[8,2,64,512]{3,2,1,0:T(8,128)(2,1)S(1)}, u32[]{:S(2)}, u32[]{:S(2)}) async-start(bf16[8,2,64,512]{3,2,1,0:T(8,128)(2,1)} %stack.2), calls=%async_computation | async-start | bytes 2097152 | tf_op jit(solution)/shard_map/all_to_all | solution.py:34
  28.0 0.0 copy-done.5
  28.0 0.6 dynamic_slice.11
  28.6 1.3 dynamic-slice
  29.9 0.0 copy-done.3
  29.9 0.2 slice_reduce_fusion.1
  30.1 0.0 copy-done.4
  30.1 0.2 select_reduce_fusion
  30.3 0.6 add_subtract_fusion
  30.9 0.0 copy-done.2
  30.9 0.2 fusion.16
  31.1 0.2 fusion.17
  31.3 54.8 %all-to-all-done = bf16[8,2,64,512]{3,2,1,0:T(8,128)(2,1)S(1)} async-done(((bf16[8,2,64,512]{3,2,1,0:T(8,128)(2,1)}), bf16[8,2,64,512]{3,2,1,0:T(8,128)(2,1)S(1)}, u32[]{:S(2)}, u32[]{:S(2)}) %all-to-all-start) | async-done | bytes 1048608 | tf_op jit(solution)/shard_map/all_to_all | solution.py:34
  86.2 0.1 copy.22
  86.3 0.3 add_convert_fusion
  86.6 87.2 %all-gather.2.cloned.1.call-done = bf16[512,8,512]{2,1,0:T(8,128)(2,1)} async-done(((bf16[8,8,512]{2,1,0:T(8,128)(2,1)}), bf16[512,8,512]{2,1,0:T(8,128)(2,1)}) %all-gather.2.cloned.1.call-update) | async-done | bytes 4194320 | tf_op jit(solution)/shard_map/all_gather | solution.py:57
  173.8 17.7 %while.11 = (s32[]{:T(128)}, f32[2,8,8]{2,1,0:T(8,128)S(1)}, bf16[8,64,8,512]{3,2,1,0:T(8,128)(2,1)}, bf16[2,512,512]{2,1,0:T(8,128)(2,1)S(1)}, s32[]{:T(128)}, /*index=5*/s32[]{:T(128)}) while((s32[]{:T(128)}, f32[2,8,8]{2,1,0:T(8,128)S(1)}, bf16[8,64,8,512]{3,2,1,0:T(8,128)(2,1)}, bf16[2,512,512]{2,1,0:T(8,128)(2,1)S(1)}, ...), condition=%wide.region_1.2_spmd.clone, body=%wide.region_0.1_spmd.clone.sunk | while | flops 545784064 | bytes 2099279 | solution.py:29
  173.8 2.2 fusion.31
  176.0 2.2 fusion.31
  178.2 2.2 fusion.31
  180.4 2.2 fusion.31
  182.7 2.2 fusion.31
  184.9 2.2 fusion.31
  187.1 2.2 fusion.31
  189.3 2.2 fusion.31
  191.5 43.0 %all-reduce = f32[2,8,8]{2,0,1:T(2,128)S(1)} all-reduce(f32[2,8,8]{2,0,1:T(2,128)S(1)} %copy.25), channel_id=2, replica_groups=mesh['pair'=64,'aux'=8] {'aux'}, use_global_device_ids=true, to_apply=%region_2.3.clone | all-reduce | flops 128 | bytes 1024
  234.6 1.2 fusion.20
  (4 shorter events, 0.0 us)
Async XLA Ops:
  6.5 1.6 copy-start
  6.5 3.5 %copy-start.1 = (bf16[2,64,512]{2,1,0:T(8,128)(2,1)S(1)}, bf16[2,64,512]{2,1,0:T(8,128)(2,1)}, u32[]{:S(2)}) copy-start(bf16[2,64,512]{2,1,0:T(8,128)(2,1)} %param.9) | copy-start | bytes 393220
  6.5 167.3 %all-gather.2.cloned.1.call-start = ((), (), s32[]{:S(2)}) async-start(), calls=%async_computation.1 | async-start | bytes 4259840 | tf_op jit(solution)/shard_map/all_gather | solution.py:57
  10.0 18.0 %copy-start.5 = (f32[8]{0:T(128)S(1)}, f32[8]{0:T(128)}, u32[]{:S(2)}) copy-start(f32[8]{0:T(128)} %param.14) | copy-start | bytes 100
  10.0 19.8 %copy-start.3 = (s32[2,2]{1,0:T(2,128)S(1)}, s32[2,2]{1,0:T(2,128)}, u32[]{:S(2)}) copy-start(s32[2,2]{1,0:T(2,128)} %param.15) | copy-start | bytes 52
  10.0 20.0 %copy-start.4 = (f32[256]{0:T(256)S(1)}, f32[256]{0:T(256)}, u32[]{:S(2)}) copy-start(f32[256]{0:T(256)} %param.13) | copy-start | bytes 3076
  10.1 20.9 %copy-start.2 = (bf16[256,512]{1,0:T(8,128)(2,1)S(1)}, bf16[256,512]{1,0:T(8,128)(2,1)}, u32[]{:S(2)}) copy-start(bf16[256,512]{1,0:T(8,128)(2,1)} %param.10) | copy-start | bytes 786436
  11.2 75.0 %all-to-all-start = ((bf16[8,2,64,512]{3,2,1,0:T(8,128)(2,1)}), bf16[8,2,64,512]{3,2,1,0:T(8,128)(2,1)S(1)}, u32[]{:S(2)}, u32[]{:S(2)}) async-start(bf16[8,2,64,512]{3,2,1,0:T(8,128)(2,1)} %stack.2), calls=%async_computation | async-start | bytes 2097152 | tf_op jit(solution)/shard_map/all_to_all | solution.py:34
Sparse Core Ops, SparseCore 0:
  10.2 163.5 all-gather.1
